TPU v7x, 32 devices: a whole 2x2x4 slice. The times are simulated.
32 devices in a mesh: pa: 4 (over x, core), pb: 8 (over z, y).
Axes of the slice: x: 2, y: 2, z: 4, core: 2. Of those that a mesh axis runs over, the one named last changes fastest.
Arguments:
- point_keys: bfloat16 [4096, 768], P(('pa', 'pb')), may hold values from -7 to 7
- point_values: bfloat16 [4096, 768], P(('pa', 'pb')), may hold values from -40 to 40
- out_grad: bfloat16 [4096, 768], P(('pa', 'pb')), may hold values from -512 to 512
- decoder_norm: float32 [12, 4096], P(None, ('pa', 'pb')), as said below
- latent_query: bfloat16 [1024, 768], P(('pa', 'pb')), may hold values from -4 to 4
- latent_out: bfloat16 [1024, 768], P(('pa', 'pb')), may hold values from -5 to 5
- encoder_norm: float32 [12, 1024], replicated, as said below
Outputs:
- keys_grad: bfloat16 [4096, 768], P(('pa', 'pb'))
- values_grad: bfloat16 [4096, 768], P(('pa', 'pb'))
- latent_grad: float32 [1024, 768], P(('pa', 'pb'))
Inputs may be any that keep to these rules, and one draw needn't show every extreme that they name: `decoder_norm`: each entry lies between log(1024) - 0.3 and log(1024) + 1.3. `encoder_norm`: each entry lies between log(4096) - 0.3 and log(4096) + 1.3.
All inputs are finite; a program needn't handle non-finite values.
Results may differ from a plain program's by a relative error of at most 0.004.
The roundings to bfloat16 on the way count: a program that leaves them out, or rounds other values in their place, can miss the bound.
Values may be sent and summed in bfloat16 or wider, within the bound.
No kernel may reach another device: no remote copies, remote signals or barrier semaphores. Data moves between devices by JAX's collectives and lax.ppermute only.
A program may use at most 64 MiB of HBM per device.

v0:
```python
import jax
import jax.numpy as jnp
from jax import lax
from jax.sharding import PartitionSpec as P

HEADS = 12
HEAD_DIM = 64


def column(block, current):
    return lax.dynamic_slice_in_dim(block, current * HEAD_DIM, HEAD_DIM, 1)


def put_head(total, piece, current):
    return lax.dynamic_update_slice_in_dim(total, piece, current * HEAD_DIM, 1)


def add_head(total, piece, current):
    return put_head(total, column(total, current) + piece, current)


def across(left, right):
    return lax.dot_general(
        left, right, (((1,), (1,)), ((), ())), preferred_element_type=jnp.float32
    )


def down_rows(left, right):
    return lax.dot_general(
        left, right, (((0,), (0,)), ((), ())), preferred_element_type=jnp.float32
    )


def shards(
    point_keys, point_values, out_grad, decoder_norm, latent_query, latent_out, encoder_norm
):
    scale_factor = HEAD_DIM ** (-0.5)
    lat_all, out_all = (
        lax.all_gather(latent_query, ("pa", "pb"), axis=0, tiled=True),
        lax.all_gather(latent_out, ("pa", "pb"), axis=0, tiled=True),
    )
    point_rows = point_keys.shape[0]
    latent_rows = lat_all.shape[0]
    width = point_keys.shape[1]

    def encoder_row(current):
        return lax.dynamic_slice_in_dim(encoder_norm, current, 1, 0)

    def pass_one(current, state):
        mix_acc, query_acc, key_acc, weighted_acc = state
        key_head = column(point_keys, current)
        grad_head = column(out_grad, current)
        lat_head = column(lat_all, current)
        scores = across(key_head, lat_head) * scale_factor
        decoder_weights = jnp.exp(scores - lax.dynamic_slice_in_dim(decoder_norm, current, 1, 0).T)
        decoder_gradient = across(grad_head, column(out_all, current))
        row_total = jnp.sum(decoder_weights * decoder_gradient, axis=1, keepdims=True)
        decoder_scores_grad = (decoder_weights * (decoder_gradient - row_total)).astype(
            jnp.bfloat16
        )
        mix_acc = put_head(
            mix_acc, down_rows(decoder_weights.astype(jnp.bfloat16), grad_head), current
        )
        query_acc = put_head(
            query_acc, down_rows(decoder_scores_grad, key_head) * scale_factor, current
        )
        key_acc = put_head(
            key_acc,
            jnp.dot(decoder_scores_grad, lat_head, preferred_element_type=jnp.float32)
            * scale_factor,
            current,
        )
        return (mix_acc, query_acc, key_acc, weighted_acc)

    weighted_blank = jnp.zeros((1, 1), jnp.float32)
    latent_blank = jnp.zeros((latent_rows, width), jnp.float32)
    begin = (
        latent_blank,
        latent_blank,
        jnp.zeros((point_rows, width), jnp.float32),
        weighted_blank,
    )
    mix_acc, query_acc, key_acc, weighted_acc = lax.fori_loop(0, HEADS, pass_one, begin)
    mix_grad = lax.psum(mix_acc, ("pa", "pb"))
    mixing_portion = mix_grad.astype(jnp.bfloat16)

    def pass_two(current, state):
        partial_rows, value_acc = state
        scores = across(column(point_keys, current), column(lat_all, current)) * scale_factor
        encoder_portion = jnp.exp(scores - encoder_row(current)).astype(jnp.bfloat16)
        mix_head = column(mixing_portion, current)
        encoder_gradient = across(column(point_values, current), mix_head)
        sums = jnp.sum(encoder_portion.astype(jnp.float32) * encoder_gradient, axis=0)[None, :]
        partial_rows = lax.dynamic_update_slice_in_dim(partial_rows, sums, current, 0)
        value_acc = put_head(
            value_acc,
            jnp.dot(encoder_portion, mix_head, preferred_element_type=jnp.float32),
            current,
        )
        return (partial_rows, value_acc)

    partial_rows, value_acc = lax.fori_loop(
        0,
        HEADS,
        pass_two,
        (jnp.zeros((HEADS, latent_rows), jnp.float32), jnp.zeros((point_rows, width), jnp.float32)),
    )
    column_total = lax.psum(partial_rows, ("pa", "pb"))

    def pass_three(current, state):
        query_acc, key_acc, value_acc = state
        key_head = column(point_keys, current)
        lat_head = column(lat_all, current)
        mix_head = column(mixing_portion, current)
        scores = across(key_head, lat_head) * scale_factor
        encoder = jnp.exp(scores - encoder_row(current))
        encoder_gradient = across(column(point_values, current), mix_head)
        encoder_scores_grad = (
            encoder * (encoder_gradient - lax.dynamic_slice_in_dim(column_total, current, 1, 0))
        ).astype(jnp.bfloat16)
        query_acc = add_head(
            query_acc, down_rows(encoder_scores_grad, key_head) * scale_factor, current
        )
        key_acc = add_head(
            key_acc,
            jnp.dot(encoder_scores_grad, lat_head, preferred_element_type=jnp.float32)
            * scale_factor,
            current,
        )
        return (query_acc, key_acc, value_acc)

    query_acc, key_acc, value_acc = lax.fori_loop(
        0, HEADS, pass_three, (query_acc, key_acc, value_acc)
    )
    latent_grad = lax.psum_scatter(query_acc, ("pa", "pb"), scatter_dimension=0, tiled=True)
    return (key_acc.astype(jnp.bfloat16), value_acc.astype(jnp.bfloat16), latent_grad)


def solution(mesh):
    in_specs = (
        P(("pa", "pb"), None),
        P(("pa", "pb"), None),
        P(("pa", "pb"), None),
        P(None, ("pa", "pb")),
        P(("pa", "pb"), None),
        P(("pa", "pb"), None),
        P(),
    )
    out_specs = (P(("pa", "pb"), None), P(("pa", "pb"), None), P(("pa", "pb"), None))
    return jax.shard_map(shards, mesh=mesh, in_specs=in_specs, out_specs=out_specs, check_vma=False)
```

profile of v0, /device:TPU:0, one launch (start us, length us, event | category | flops | bytes accessed | tf_op | source)
XLA Modules:
  0.0 576.5 jit_solution(12292148037386380637)
XLA Ops:
  9.4 59.3 %all-gather.3.cloned.1.call-done = bf16[1024,768]{1,0:T(8,128)(2,1)} async-done(((bf16[32,768]{1,0:T(8,128)(2,1)}), bf16[1024,768]{1,0:T(8,128)(2,1)}) %all-gather.3.cloned.1.call-update) | async-done | bytes 1572880 | tf_op jit(solution)/shard_map/all_gather | solution.py:39
  68.7 56.9 %all-gather.5.cloned.1.call-done = bf16[1024,768]{1,0:T(8,128)(2,1)} async-done(((bf16[32,768]{1,0:T(8,128)(2,1)}), bf16[1024,768]{1,0:T(8,128)(2,1)}) %all-gather.5.cloned.1.call-update) | async-done | bytes 1572880 | tf_op jit(solution)/shard_map/all_gather | solution.py:40
  125.5 2.0 broadcast_in_dim.16
  127.6 2.1 broadcast_in_dim.16.clone
  129.7 86.6 %while.47 = (s32[]{:T(128)}, f32[1024,768]{0,1:T(8,128)}, f32[1024,768]{0,1:T(8,128)}, f32[128,768]{0,1:T(8,128)S(1)}, bf16[128,768]{1,0:T(8,128)(2,1)}, /*index...) while((s32[]{:T(128)}, f32[1024,768]{0,1:T(8,128)}, ...), condition=%wide.region_2.0_spmd, body=%wide.region_0.0_spmd.sunk | while | flops 85008256 | bytes 5414575 | solution.py:83
  163.6 1.8 convolution_dynamic-update-slice_fusion.4
  170.8 1.8 convolution_dynamic-update-slice_fusion.4
  190.6 1.8 fusion.95
  192.4 1.8 convolution_dynamic-update-slice_fusion.4
  197.9 1.8 fusion.95
  205.1 1.8 fusion.95
  212.4 1.8 fusion.95
  214.1 1.8 convolution_dynamic-update-slice_fusion.4
  216.3 3.6 copy.10
  219.9 76.8 %all-reduce.1 = bf16[1024,768]{1,0:T(8,128)(2,1)S(1)} all-reduce(f32[1024,768]{1,0:T(8,128)} %copy.10), channel_id=1, replica_groups=mesh['pa'=4,'pb'=8] {'pa','pb'}, use_global_device_ids=true, to_apply=%region_3.0 | all-reduce | flops 786432 | bytes 4718592 | tf_op jit(solution)/shard_map/psum | solution.py:84
  296.7 64.0 %while.48 = (s32[]{:T(128)}, f32[12,1024]{1,0:T(8,128)}, bf16[128,768]{0,1:T(8,128)(2,1)}, bf16[128,768]{1,0:T(8,128)(2,1)}, bf16[1024,768]{1,0:T(8,128)(2,1)S(1...) while((s32[]{:T(128)}, f32[12,1024]{1,0:T(8,128)}, ...), condition=%wide.region_6.0_spmd, body=%wide.region_4.0_spmd.sunk | while | flops 51117060 | bytes 1698987 | solution.py:102
  360.7 39.1 %psum.15 = f32[12,1024]{1,0:T(8,128)} all-reduce(f32[12,1024]{1,0:T(8,128)} %get-tuple-element.457), channel_id=1, replica_groups=mesh['pa'=4,'pb'=8] {'pa','pb'}, use_global_device_ids=true, to_apply=%region_7.0 | all-reduce | flops 12288 | bytes 98304 | tf_op jit(solution)/shard_map/psum | solution.py:108
  399.8 64.4 %while.49 = (s32[]{:T(128)}, f32[1024,768]{0,1:T(8,128)}, f32[128,768]{0,1:T(8,128)S(1)}, bf16[128,768]{1,0:T(8,128)(2,1)}, bf16[1024,768]{1,0:T(8,128)(2,1)S(1)...) while((s32[]{:T(128)}, f32[1024,768]{0,1:T(8,128)}, ...), condition=%wide.region_9.0_spmd, body=%wide.region_8.0_spmd.sunk | while | flops 67911680 | bytes 3338415 | solution.py:132
  402.8 2.0 fusion.114
  408.1 2.0 fusion.114
  413.5 2.0 fusion.114
  418.8 2.0 fusion.114
  424.2 2.0 fusion.114
  429.5 2.0 fusion.114
  434.9 2.0 fusion.114
  440.3 2.0 fusion.114
  445.6 2.0 fusion.114
  451.0 2.0 fusion.114
  456.4 2.0 fusion.114
  461.8 2.0 fusion.114
  464.1 3.5 copy.13
  469.4 100.6 %reduce-scatter.2.cloned.1.call-done = f32[32,768]{1,0:T(8,128)} async-done(((f32[1024,768]{1,0:T(8,128)}), f32[32,768]{1,0:T(8,128)}) %reduce-scatter.2.cloned.1.call-update) | async-done | bytes 98320 | tf_op jit(solution)/shard_map/reduce_scatter | solution.py:135
  (199 shorter events, 179.6 us)
Async XLA Ops:
  7.2 61.5 %all-gather.3.cloned.1.call-start = ((), (), s32[]{:S(2)}) async-start(), calls=%async_computation.1 | async-start | bytes 1622016 | tf_op jit(solution)/shard_map/all_gather | solution.py:39
  7.9 117.6 %all-gather.5.cloned.1.call-start = ((), (), s32[]{:S(2)}) async-start(), calls=%async_computation.2 | async-start | bytes 1622016 | tf_op jit(solution)/shard_map/all_gather | solution.py:40
  8.6 561.4 %reduce-scatter.2.cloned.1.call-start = ((), (), s32[]{:S(2)}) async-start(), calls=%async_computation.3 | async-start | bytes 3244032 | tf_op jit(solution)/shard_map/reduce_scatter | solution.py:135
  68.7 61.0 %copy-start = (bf16[1024,768]{1,0:T(8,128)(2,1)S(1)}, bf16[1024,768]{1,0:T(8,128)(2,1)}, u32[]{:S(2)}) copy-start(bf16[1024,768]{1,0:T(8,128)(2,1)} %all-gather.3.cloned.1.call-done) | copy-start | bytes 4718596
  467.7 0.9 copy-start.1
Sparse Core Ops, SparseCore 0:
  10.9 57.7 all-gather.2
  71.6 53.9 all-gather.4
  467.8 102.1 reduce-scatter.1
where the time goes:
time: 586 us; the launch traced here: 577 us
  waiting for transfers between devices  218 us (37%)
  matrix products  168 us (29%)
  blocking collectives  116 us (20%)
  local copies, waits for them, and re-layouts  56.8 us (10%)
  between operations  13.8 us (2%)
    reduce_scatter x1, waiting for transfers between devices, shards(): lax.psum_scatter(query_acc, ('pa', 'pb'), scatter_dimension=0, tiled=True)  101 us
    dot_general x72, matrix products, across(): lax.dot_general(left, right, (((1,), (1,)), ((), ())), preferred_element_...  81.6 us
    psum x1, blocking collectives, shards(): mix_grad = lax.psum(mix_acc, ('pa', 'pb'))  76.8 us
    dot_general x36, matrix products, down_rows(): lax.dot_general(left, right, (((0,), (0,)), ((), ())), preferred_element_...  66.1 us
    all_gather x1, waiting for transfers between devices, shards(): lax.all_gather(latent_query, ('pa', 'pb'), axis=0, tiled=True)  59.3 us
    all_gather x1, waiting for transfers between devices, shards(): lax.all_gather(latent_out, ('pa', 'pb'), axis=0, tiled=True)  56.9 us
    psum x1, blocking collectives, shards(): column_total = lax.psum(partial_rows, ('pa', 'pb'))  39.1 us
    dynamic_slice x24, local copies, waits for them, and re-layouts, encoder_row(): return lax.dynamic_slice_in_dim(encoder_norm, current, 1, 0)  18.6 us
  transfers between devices with their start and end apart: 3, of which 3 were waited for; matrix products, arithmetic and copies ran while one was open for 0% of the time, Pallas kernels for 0%

commit v1 on v0

--- a/solution.py
+++ b/solution.py
@@ -81,7 +81,8 @@
         weighted_blank,
     )
     mix_acc, query_acc, key_acc, weighted_acc = lax.fori_loop(0, HEADS, pass_one, begin)
-    mix_grad = lax.psum(mix_acc, ("pa", "pb"))
+    recover_gates_by_axis = lambda xs: lax.psum(lax.psum(xs, "pb"), axis_name="pa")
+    mix_grad = recover_gates_by_axis(mix_acc)
     mixing_portion = mix_grad.astype(jnp.bfloat16)
 
     def pass_two(current, state):

time: 586 us -> 702 us (1.20)
  waiting for transfers between devices: 218 us -> 346 us
  blocking collectives: 116 us -> 98.9 us
    psum x0 -> x1, waiting for transfers between devices: none -> 127 us  [shards(): lax.psum(xs, 'pb')]
    psum x1, blocking collectives: 76.8 us -> 58.8 us  [shards(): lax.psum(lax.psum(xs, 'pb'), axis_name='pa')]
    dot_general x12, matrix products: 4.43 us -> 15.8 us  [pass_one(): jnp.dot(decoder_scores_grad, lat_head, preferred_element_type=jnp.float32)]
    dot_general x36, matrix products: 66.1 us -> 57.7 us  [down_rows(): lax.dot_general(left, right, (((0,), (0,)), ((), ())), preferred_element_...]
  transfers between devices with their start and end apart: 3 -> 4, of which waited for: 3 -> 4; matrix products, arithmetic and copies ran while one was open for 0% -> 0% of each run, Pallas kernels for 0% -> 0%
where the time goes in v1:
time: 702 us; the launch traced here: 693 us
  waiting for transfers between devices  346 us (49%)
  matrix products  174 us (25%)
  blocking collectives  98.9 us (14%)
  local copies, waits for them, and re-layouts  56.3 us (8%)
  between operations  13.8 us (2%)
    psum x1, waiting for transfers between devices, shards(): lax.psum(xs, 'pb')  127 us
    reduce_scatter x1, waiting for transfers between devices, shards(): lax.psum_scatter(query_acc, ('pa', 'pb'), scatter_dimension=0, tiled=True)  101 us
    dot_general x72, matrix products, across(): lax.dot_general(left, right, (((1,), (1,)), ((), ())), preferred_element_...  84.2 us
    all_gather x1, waiting for transfers between devices, shards(): lax.all_gather(latent_query, ('pa', 'pb'), axis=0, tiled=True)  60 us
    psum x1, blocking collectives, shards(): lax.psum(lax.psum(xs, 'pb'), axis_name='pa')  58.8 us
    dot_general x36, matrix products, down_rows(): lax.dot_general(left, right, (((0,), (0,)), ((), ())), preferred_element_...  57.7 us
    all_gather x1, waiting for transfers between devices, shards(): lax.all_gather(latent_out, ('pa', 'pb'), axis=0, tiled=True)  56.9 us
    psum x1, blocking collectives, shards(): column_total = lax.psum(partial_rows, ('pa', 'pb'))  40.1 us
  transfers between devices with their start and end apart: 4, of which 4 were waited for; matrix products, arithmetic and copies ran while one was open for 0% of the time, Pallas kernels for 0%

profile of v1, /device:TPU:0, one launch (start us, length us, event | category | flops | bytes accessed | tf_op | source)
XLA Modules:
  0.0 692.7 jit_solution(8703374157869304728)
XLA Ops:
  8.7 60.0 %all-gather.3.cloned.1.call-done = bf16[1024,768]{1,0:T(8,128)(2,1)} async-done(((bf16[32,768]{1,0:T(8,128)(2,1)}), bf16[1024,768]{1,0:T(8,128)(2,1)}) %all-gather.3.cloned.1.call-update) | async-done | bytes 1572880 | tf_op jit(solution)/shard_map/all_gather | solution.py:39
  68.7 56.9 %all-gather.5.cloned.1.call-done = bf16[1024,768]{1,0:T(8,128)(2,1)} async-done(((bf16[32,768]{1,0:T(8,128)(2,1)}), bf16[1024,768]{1,0:T(8,128)(2,1)}) %all-gather.5.cloned.1.call-update) | async-done | bytes 1572880 | tf_op jit(solution)/shard_map/all_gather | solution.py:40
  125.5 2.1 broadcast_in_dim.16
  128.1 92.3 %while.47 = (s32[]{:T(128)}, f32[1024,768]{0,1:T(8,128)}, f32[1024,768]{0,1:T(8,128)S(1)}, f32[128,768]{0,1:T(8,128)S(1)}, bf16[128,768]{1,0:T(8,128)(2,1)}, /*i...) while((s32[]{:T(128)}, f32[1024,768]{0,1:T(8,128)}, ...), condition=%wide.region_2.0_spmd, body=%wide.region_0.0_spmd.sunk | while | flops 85008256 | bytes 5414575 | solution.py:83
  132.7 1.8 convolution_dynamic-update-slice_fusion.4
  148.0 1.8 convolution_dynamic-update-slice_fusion.4
  155.7 1.8 convolution_dynamic-update-slice_fusion.4
  186.5 1.8 convolution_dynamic-update-slice_fusion.4
  194.2 1.8 convolution_dynamic-update-slice_fusion.4
  201.9 1.8 convolution_dynamic-update-slice_fusion.4
  209.6 1.8 convolution_dynamic-update-slice_fusion.4
  217.3 1.8 convolution_dynamic-update-slice_fusion.4
  220.4 4.7 copy.10
  225.9 127.1 %all-reduce.3.cloned.1.call-done = f32[1024,768]{1,0:T(8,128)} async-done(((f32[1024,768]{1,0:T(8,128)}), f32[1024,768]{1,0:T(8,128)}) %all-reduce.3.cloned.1.call-update) | async-done | bytes 3145744 | tf_op jit(solution)/shard_map/psum | solution.py:84
  352.9 58.8 %all-reduce.4 = bf16[1024,768]{1,0:T(8,128)(2,1)S(1)} all-reduce(f32[1024,768]{1,0:T(8,128)} %all-reduce.3.cloned.1.call-done), channel_id=1, replica_groups=mesh['pa'=4,'pb'=8] {'pa'}, use_global_device_ids=true, to_apply=%region_4.0 | all-reduce | flops 786432 | bytes 4718592 | tf_op jit(solution)/shard_map/psum | solution.py:84
  411.7 64.0 %while.48 = (s32[]{:T(128)}, f32[12,1024]{1,0:T(8,128)}, bf16[128,768]{0,1:T(8,128)(2,1)}, bf16[128,768]{1,0:T(8,128)(2,1)}, bf16[1024,768]{1,0:T(8,128)(2,1)S(1...) while((s32[]{:T(128)}, f32[12,1024]{1,0:T(8,128)}, ...), condition=%wide.region_7.0_spmd, body=%wide.region_5.0_spmd.sunk | while | flops 51117060 | bytes 1698987 | solution.py:103
  475.7 40.1 %psum.23 = f32[12,1024]{1,0:T(8,128)} all-reduce(f32[12,1024]{1,0:T(8,128)} %get-tuple-element.457), channel_id=1, replica_groups=mesh['pa'=4,'pb'=8] {'pa','pb'}, use_global_device_ids=true, to_apply=%region_8.0 | all-reduce | flops 12288 | bytes 98304 | tf_op jit(solution)/shard_map/psum | solution.py:109
  515.8 64.4 %while.49 = (s32[]{:T(128)}, f32[1024,768]{0,1:T(8,128)}, f32[128,768]{0,1:T(8,128)S(1)}, bf16[128,768]{1,0:T(8,128)(2,1)}, bf16[1024,768]{1,0:T(8,128)(2,1)S(1)...) while((s32[]{:T(128)}, f32[1024,768]{0,1:T(8,128)}, ...), condition=%wide.region_10.0_spmd, body=%wide.region_9.0_spmd.sunk | while | flops 67911680 | bytes 3338415 | solution.py:133
  518.8 2.0 fusion.114
  524.1 2.0 fusion.114
  529.5 2.0 fusion.114
  534.8 2.0 fusion.114
  540.2 2.0 fusion.114
  545.6 2.0 fusion.114
  550.9 2.0 fusion.114
  556.3 2.0 fusion.114
  561.6 2.0 fusion.114
  567.0 2.0 fusion.114
  572.4 2.0 fusion.114
  577.8 2.0 fusion.114
  580.2 3.6 copy.13
  585.5 100.7 %reduce-scatter.2.cloned.1.call-done = f32[32,768]{1,0:T(8,128)} async-done(((f32[1024,768]{1,0:T(8,128)}), f32[32,768]{1,0:T(8,128)}) %reduce-scatter.2.cloned.1.call-update) | async-done | bytes 98320 | tf_op jit(solution)/shard_map/reduce_scatter | solution.py:136
  (204 shorter events, 185.7 us)
Async XLA Ops:
  7.2 61.5 %all-gather.3.cloned.1.call-start = ((), (), s32[]{:S(2)}) async-start(), calls=%async_computation.1 | async-start | bytes 1622016 | tf_op jit(solution)/shard_map/all_gather | solution.py:39
  7.9 117.6 %all-gather.5.cloned.1.call-start = ((), (), s32[]{:S(2)}) async-start(), calls=%async_computation.2 | async-start | bytes 1622016 | tf_op jit(solution)/shard_map/all_gather | solution.py:40
  8.6 344.3 %all-reduce.3.cloned.1.call-start = ((), (), s32[]{:S(2)}) async-start(), calls=%async_computation.3 | async-start | bytes 6291456 | tf_op jit(solution)/shard_map/psum | solution.py:84
  220.4 4.7 copy-start
  225.1 186.6 %copy-start.1 = (bf16[1024,768]{1,0:T(8,128)(2,1)S(1)}, bf16[1024,768]{1,0:T(8,128)(2,1)}, u32[]{:S(2)}) copy-start(bf16[1024,768]{1,0:T(8,128)(2,1)} %get-tuple-element.804) | copy-start | bytes 4718596
  225.1 461.0 %reduce-scatter.2.cloned.1.call-start = ((), (), s32[]{:S(2)}) async-start(), calls=%async_computation.4 | async-start | bytes 3244032 | tf_op jit(solution)/shard_map/reduce_scatter | solution.py:136
  583.7 0.9 copy-start.2
Sparse Core Ops, SparseCore 0:
  10.9 57.7 all-gather.2
  71.6 53.9 all-gather.4
  225.2 127.6 all-reduce.2
  583.9 102.2 reduce-scatter.1
